TPU v7x, 256 devices: a whole 4x4x8 slice. The times are simulated.
256 devices in a mesh: dp: 32 (over z, x_lo, core), shard: 8 (over y, x_hi).
Axes of the slice: x: 4 (x_hi: 2, x_lo: 2; x = x_hi * 2 + x_lo), y: 4, z: 8, core: 2. Of those that a mesh axis runs over, the one named last changes fastest.
Arguments:
- acts: bfloat16 [65536, 4096], P('dp', 'shard'), may hold values from -6 to 6
- grad_out: bfloat16 [65536, 14336], P('dp', 'shard'), may hold values from -15 to 15
- projector: bfloat16 [4096, 512], P('shard'), may hold values from -0.09375 to 0.09375
- weight: bfloat16 [4096, 14336], P('dp', 'shard'), may hold values from -0.09375 to 0.09375
- moment1: float32 [512, 14336], P('dp', 'shard'), may hold values from -24 to 24
- moment2: float32 [512, 14336], P('dp', 'shard'), may hold values from 1 to 16
Outputs:
- new_weight: bfloat16 [4096, 14336], P('dp', 'shard')
- new_moment1: float32 [512, 14336], P('dp', 'shard')
- new_moment2: float32 [512, 14336], P('dp', 'shard')
All inputs are finite; a program needn't handle non-finite values.
Results may differ from a plain program's by a relative error of at most 0.005.
Values may be sent and summed in bfloat16 or wider, within the bound.
A program may use at most 64 MiB of HBM per device.

v0:
```python
import functools

import jax
import jax.numpy as jnp
from jax import lax
from jax.sharding import Mesh
from jax.sharding import PartitionSpec as P

FF = 14336
R = 512
SHARD = ("shard_0", "shard_1")
DP = ("dp_0", "dp_1", "dp_2")
DP_SHARD = ("dp_0", "dp_1", "dp_2", "shard_0", "shard_1")


first_fix = 0.9999734386011124
second_fix = 0.994079470779666


def scatter_axes(array, axes, dim):
    if not axes:
        return array
    nearer = lax.psum_scatter(array, axes[0], scatter_dimension=dim, tiled=True)
    return scatter_axes(nearer, axes[1:], dim)


def sent_to_all(array, axis):
    copies = jnp.broadcast_to(array, (lax.axis_size(axis), *array.shape))
    return lax.all_to_all(copies, axis, split_axis=0, concat_axis=0, tiled=True)


def joined_along(pieces, dim):
    pieces = jnp.moveaxis(pieces, 0, dim)
    shape = pieces.shape
    return pieces.reshape(*shape[:dim], shape[dim] * shape[dim + 1], *shape[dim + 2 :])


def collect(array, axis, dim):
    pieces = sent_to_all(array, axis)
    return joined_along(pieces, dim)


def in_blocks(array, dim, count):
    before, after = (array.shape[:dim], array.shape[dim + 1 :])
    return jnp.moveaxis(array.reshape(*before, count, -1, *after), dim, 0)


def sent_and_summed(array, axis, dim):
    count = lax.axis_size(axis)
    pieces = lax.all_to_all(in_blocks(array, dim, count), axis, 0, 0, tiled=True)
    return jnp.sum(pieces, axis=0)


def summed_rows(array, axes, dim):
    far, near = axes
    own = sent_and_summed(in_blocks(array, dim, lax.axis_size(far)), near, dim + 1)
    return jnp.sum(lax.all_to_all(own, far, 0, 0, tiled=True), axis=0)


def one_axis_at_a_time(array, axes):
    return functools.reduce(lax.psum, axes, array)


def broadcast(array, axis, root):
    return lax.dynamic_index_in_dim(lax.all_gather(array, axis), root, 0, keepdims=False)


def whole_of(array, axes, dim):
    far, near = axes
    pieces = sent_to_all(sent_to_all(array, far), near)
    return joined_along(pieces.swapaxes(0, 1).reshape(-1, *array.shape), dim)


def token_product(projected_rows, grad_rows):
    return lax.dot_general(
        projected_rows, grad_rows, (((0,), (0,)), ((), ())), preferred_element_type=jnp.float32
    )


def body(acts, grad_out, projector, weight, moment1, moment2):
    partial_acts = jnp.dot(acts, projector, preferred_element_type=jnp.float32)
    token_share = scatter_axes(partial_acts, SHARD, 0).astype(jnp.bfloat16)
    group_grad = token_product(collect(token_share, SHARD, 0), grad_out)
    gradient = summed_rows(group_grad, (("dp_0", "dp_1"), "dp_2"), 0)
    square_sum = one_axis_at_a_time(jnp.sum(gradient * gradient), DP_SHARD)
    root_mean = jnp.sqrt(square_sum / (R * FF) + 1e-06)
    clip_factor = jnp.minimum(1.0, 4.0 / root_mean)
    clipped = clip_factor * gradient
    new_moment1 = 0.9 * moment1 + 0.1 * clipped
    new_moment2 = 0.95 * moment2 + 0.05 * clipped * clipped
    update = (new_moment1 / first_fix / (jnp.sqrt(new_moment2 / second_fix) + 1e-08)).astype(
        jnp.bfloat16
    )
    weight_rows = weight.shape[0]
    basis_count = projector.shape[0]
    dp_index = lax.axis_index(DP)
    holder = dp_index * weight_rows // basis_count
    offset = dp_index * weight_rows - holder * basis_count
    candidate = lax.dynamic_slice_in_dim(projector, offset, weight_rows, 0)
    basis = broadcast(candidate, SHARD, holder)
    change_sum = jnp.dot(
        basis, whole_of(update, (("dp_0", "dp_1"), "dp_2"), 0), preferred_element_type=jnp.float32
    )
    new_weight = (weight.astype(jnp.float32) - 0.2 * change_sum).astype(jnp.bfloat16)
    return (new_weight, new_moment1, new_moment2)


def solution(mesh):
    finer = Mesh(
        mesh.devices.reshape(8, 2, 2, 4, 2), ("dp_0", "dp_1", "dp_2", "shard_0", "shard_1")
    )
    in_specs = (
        P(DP, SHARD),
        P(DP, SHARD),
        P(SHARD, None),
        P(DP, SHARD),
        P(DP, SHARD),
        P(DP, SHARD),
    )
    out_specs = (P(DP, SHARD), P(DP, SHARD), P(DP, SHARD))
    return jax.shard_map(body, mesh=finer, in_specs=in_specs, out_specs=out_specs, check_vma=False)
```

profile of v0, /device:TPU:1, one launch (start us, length us, event | category | flops | bytes accessed | tf_op | source)
XLA Modules:
  0.0 305.1 jit_solution(1758720004445559638)
XLA Ops:
  8.0 0.0 copy-start
  8.0 0.0 reduce-scatter.3.cloned.1.call-start
  8.1 1.5 copy-done
  9.6 4.2 %fusion.12 = f32[2048,512]{1,0:T(8,128)} fusion(bf16[2048,512]{1,0:T(8,128)(2,1)S(1)} %copy-done, bf16[512,512]{1,0:T(8,128)(2,1)} %param.8), kind=kOutput, calls=%fused_computation.15 | convolution fusion | flops 1073741824 | bytes 6815744 | tf_op jit(solution)/shard_map/dot_general | solution.py:81
  13.8 0.0 reduce-scatter.3.cloned.1.call-update
  13.8 0.0 reduce-scatter.5.cloned.1.call-start
  13.9 53.4 %reduce-scatter.3.cloned.1.call-done = f32[512,512]{1,0:T(8,128)} async-done(((f32[2048,512]{1,0:T(8,128)}), f32[512,512]{1,0:T(8,128)}) %reduce-scatter.3.cloned.1.call-update) | async-done | bytes 1048592 | tf_op jit(solution)/shard_map/reduce_scatter | solution.py:23
  67.2 0.0 reduce-scatter.5.cloned.1.call-update
  67.3 29.2 %reduce-scatter.5.cloned.1.call-done = f32[256,512]{1,0:T(8,128)} async-done(((f32[512,512]{1,0:T(8,128)}), f32[256,512]{1,0:T(8,128)}) %reduce-scatter.5.cloned.1.call-update) | async-done | bytes 524304 | tf_op jit(solution)/shard_map/reduce_scatter | solution.py:23
  96.5 1.1 convert_element_type.13
  97.6 0.1 copy.19
  97.7 0.1 broadcast_in_dim.9
  97.9 31.4 %all_to_all.25 = bf16[8,256,512]{1,2,0:T(8,128)(2,1)} all-to-all(bf16[8,256,512]{1,2,0:T(8,128)(2,1)S(1)} %broadcast_in_dim.9), channel_id=1, replica_groups=mesh['dp_0'=8,'dp_1'=2,'dp_2'=2,'shard_0'=4,'shard_1'=2] {'shard_0','sha..., dimensions={0} | all-to-all | bytes 4194304 | tf_op jit(solution)/shard_map/all_to_all | solution.py:29
  129.3 3.9 %copy.20 = bf16[8,256,512]{2,1,0:T(8,128)(2,1)} copy(bf16[8,256,512]{1,2,0:T(8,128)(2,1)} %all_to_all.25) | data formatting | bytes 4194304 | tf_op jit(solution)/shard_map/all_to_all | solution.py:29
  133.2 4.0 %copy.21 = bf16[512,2048]{1,0:T(8,128)(2,1)} copy(bf16[512,2048]{0,1:T(8,128)(2,1)} %bitcast.24) | data formatting | bytes 4194304 | tf_op jit(solution)/shard_map/dot_general | solution.py:75
  137.2 7.7 %fusion.2 = f32[2,16,16,1792]{3,2,0,1:T(8,128)S(1)} fusion(bf16[16,2,16,2048]{3,2,1,0:T(8,128)(2,1)} %bitcast.26, bf16[2048,1792]{1,0:T(8,128)(2,1)} %param.7), kind=kOutput, calls=%fused_computation.2 | convolution fusion | flops 3758096384 | bytes 13107200 | tf_op jit(solution)/shard_map/dot_general | solution.py:75
  144.9 0.3 copy.22
  145.2 9.2 %all_to_all.26 = f32[2,16,16,1792]{3,2,1,0:T(8,128)} all-to-all(f32[2,16,16,1792]{3,2,1,0:T(8,128)S(1)} %copy.22), channel_id=1, replica_groups=mesh['dp_0'=8,'dp_1'=2,'dp_2'=2,'shard_0'=4,'shard_1'=2] {'dp_2'}, dimensions={0} | all-to-all | bytes 7340032 | tf_op jit(solution)/shard_map/all_to_all | solution.py:50
  154.4 3.7 %reduce_sum.27 = f32[16,16,1792]{2,1,0:T(8,128)} reduce(f32[2,16,16,1792]{3,2,1,0:T(8,128)} %all_to_all.26, f32[]{:T(128)} %constant.62.clone.1), dimensions={0}, to_apply=%region_2.0 | reduce | flops 458752 | bytes 5505028 | tf_op jit(solution)/shard_map/reduce_sum | solution.py:51
  158.1 8.0 %all-to-all-start.2 = ((f32[16,16,1792]{2,1,0:T(8,128)}), f32[16,16,1792]{2,1,0:T(8,128)}, u32[]{:S(2)}, u32[]{:S(2)}) async-start(f32[16,16,1792]{2,1,0:T(8,128)} %reduce_sum.27), calls=%async_computation.4 | async-start | bytes 3670016 | tf_op jit(solution)/shard_map/all_to_all | solution.py:57
  166.2 0.0 copy-start.2
  166.2 0.0 copy-start.3
  166.2 0.0 all-gather.3.cloned.1.call-start
  166.3 42.7 %all-to-all-done.2 = f32[16,16,1792]{2,1,0:T(8,128)} async-done(((f32[16,16,1792]{2,1,0:T(8,128)}), f32[16,16,1792]{2,1,0:T(8,128)}, u32[]{:S(2)}, u32[]{:S(2)}) %all-to-all-start.2) | async-done | bytes 1835040 | tf_op jit(solution)/shard_map/all_to_all | solution.py:57
  208.9 1.6 reduce_sum.28
  210.5 0.6 multiply_reduce_fusion
  211.2 14.0 %psum.35 = f32[]{:T(128)} all-reduce(f32[]{:T(128)} %multiply_reduce_fusion), channel_id=1, replica_groups=mesh['dp_0'=8,'dp_1'=2,'dp_2'=2,'shard_0'=4,'shard_1'=2] {'dp_0'}, use_global_device_ids=true, to_apply=%region_5.0 | all-reduce | flops 1 | bytes 8 | tf_op jit(solution)/shard_map/psum | solution.py:61
  225.2 4.4 %psum.36 = f32[]{:T(128)} all-reduce(f32[]{:T(128)} %psum.35), channel_id=1, replica_groups=mesh['dp_0'=8,'dp_1'=2,'dp_2'=2,'shard_0'=4,'shard_1'=2] {'dp_1'}, use_global_device_ids=true, to_apply=%region_6.0 | all-reduce | flops 1 | bytes 8 | tf_op jit(solution)/shard_map/psum | solution.py:61
  229.6 7.8 %psum.37 = f32[]{:T(128)} all-reduce(f32[]{:T(128)} %psum.36), channel_id=1, replica_groups=mesh['dp_0'=8,'dp_1'=2,'dp_2'=2,'shard_0'=4,'shard_1'=2] {'dp_2'}, use_global_device_ids=true, to_apply=%region_7.0 | all-reduce | flops 1 | bytes 8 | tf_op jit(solution)/shard_map/psum | solution.py:61
  237.4 1.6 constant_dynamic-slice_fusion
  239.0 7.1 %psum.38 = f32[]{:T(128)} all-reduce(f32[]{:T(128)} %psum.37), channel_id=1, replica_groups=mesh['dp_0'=8,'dp_1'=2,'dp_2'=2,'shard_0'=4,'shard_1'=2] {'shard_0'}, use_global_device_ids=true, to_apply=%region_8.0 | all-reduce | flops 1 | bytes 8 | tf_op jit(solution)/shard_map/psum | solution.py:61
  246.1 0.0 all-gather.3.cloned.1.call-update
  246.1 5.9 %psum.39 = f32[]{:T(128)} all-reduce(f32[]{:T(128)} %psum.38), channel_id=1, replica_groups=mesh['dp_0'=8,'dp_1'=2,'dp_2'=2,'shard_0'=4,'shard_1'=2] {'shard_1'}, use_global_device_ids=true, to_apply=%region_9.0 | all-reduce | flops 1 | bytes 8 | tf_op jit(solution)/shard_map/psum | solution.py:61
  252.7 0.0 copy-done.2
  252.7 0.0 copy-done.3
  252.7 0.8 divide_convert_fusion
  253.5 1.0 broadcast_in_dim.10
  254.5 5.8 %all-to-all-start.3 = ((bf16[16,16,1792]{2,1,0:T(8,128)(2,1)}), bf16[16,16,1792]{2,1,0:T(8,128)(2,1)S(1)}, u32[]{:S(2)}, u32[]{:S(2)}) async-start(bf16[16,16,1792]{2,1,0:T(8,128)(2,1)} %broadcast_in_dim.10), calls=%async_computation.5 | async-start | bytes 1835008 | tf_op jit(solution)/shard_map/all_to_all | solution.py:29
  260.3 21.9 %all-to-all-done.3 = bf16[16,16,1792]{2,1,0:T(8,128)(2,1)S(1)} async-done(((bf16[16,16,1792]{2,1,0:T(8,128)(2,1)}), bf16[16,16,1792]{2,1,0:T(8,128)(2,1)S(1)}, u32[]{:S(2)}, u32[]{:S(2)}) %all-to-all-start.3) | async-done | bytes 917536 | tf_op jit(solution)/shard_map/all_to_all | solution.py:29
  282.2 0.1 broadcast_in_dim.11
  282.3 9.2 %all_to_all.27 = bf16[2,16,16,1792]{3,2,1,0:T(8,128)(2,1)S(1)} all-to-all(bf16[2,16,16,1792]{3,2,1,0:T(8,128)(2,1)S(1)} %broadcast_in_dim.11), channel_id=1, replica_groups=mesh['dp_0'=8,'dp_1'=2,'dp_2'=2,'shard_0'=4,'shard_1'=2] {'dp_2'}, dimensions={0} | all-to-all | bytes 3670016 | tf_op jit(solution)/shard_map/all_to_all | solution.py:29
  291.5 0.0 copy-start.1
  291.5 1.5 copy.23
  293.0 1.9 all-gather.3.cloned.1.call-done
  294.9 0.0 copy-done.1
  294.9 2.8 fusion.6
Async XLA Ops:
  8.0 1.6 copy-start
  8.0 59.2 %reduce-scatter.3.cloned.1.call-start = ((), (), s32[]{:S(2)}) async-start(), calls=%async_computation.7 | async-start | bytes 5242880 | tf_op jit(solution)/shard_map/reduce_scatter | solution.py:23
  13.8 82.7 %reduce-scatter.5.cloned.1.call-start = ((), (), s32[]{:S(2)}) async-start(), calls=%async_computation.8 | async-start | bytes 1572864 | tf_op jit(solution)/shard_map/reduce_scatter | solution.py:23
  158.1 50.8 %all-to-all-start.2 = ((f32[16,16,1792]{2,1,0:T(8,128)}), f32[16,16,1792]{2,1,0:T(8,128)}, u32[]{:S(2)}, u32[]{:S(2)}) async-start(f32[16,16,1792]{2,1,0:T(8,128)} %reduce_sum.27), calls=%async_computation.4 | async-start | bytes 3670016 | tf_op jit(solution)/shard_map/all_to_all | solution.py:57
  166.2 86.6 %copy-start.2 = (f32[16,1792]{1,0:T(8,128)S(1)}, f32[16,1792]{1,0:T(8,128)}, u32[]{:S(2)}) copy-start(f32[16,1792]{1,0:T(8,128)} %param.10) | copy-start | bytes 344068
  166.2 86.6 %copy-start.3 = (f32[16,1792]{1,0:T(8,128)S(1)}, f32[16,1792]{1,0:T(8,128)}, u32[]{:S(2)}) copy-start(f32[16,1792]{1,0:T(8,128)} %param.11) | copy-start | bytes 344068
  166.2 128.8 %all-gather.3.cloned.1.call-start = ((), (), s32[]{:S(2)}) async-start(), calls=%async_computation.9 | async-start | bytes 1179648 | tf_op jit(solution)/shard_map/all_gather | solution.py:65
  254.5 27.7 %all-to-all-start.3 = ((bf16[16,16,1792]{2,1,0:T(8,128)(2,1)}), bf16[16,16,1792]{2,1,0:T(8,128)(2,1)S(1)}, u32[]{:S(2)}, u32[]{:S(2)}) async-start(bf16[16,16,1792]{2,1,0:T(8,128)(2,1)} %broadcast_in_dim.10), calls=%async_computation.5 | async-start | bytes 1835008 | tf_op jit(solution)/shard_map/all_to_all | solution.py:29
  291.5 3.4 %copy-start.1 = (bf16[128,1792]{1,0:T(8,128)(2,1)S(1)}, bf16[128,1792]{1,0:T(8,128)(2,1)}, u32[]{:S(2)}) copy-start(bf16[128,1792]{1,0:T(8,128)(2,1)} %param.9) | copy-start | bytes 1376260
Sparse Core Ops, SparseCore 0:
  14.0 53.2 reduce-scatter.2
  69.9 26.5 reduce-scatter.4
Sparse Core Ops, SparseCore 1:
  246.2 48.7 all-gather.2
where the time goes:
time: 306 us; the launch traced here: 305 us
  waiting for transfers between devices  149 us (49%)
  blocking collectives  89.1 us (29%)
  between operations  16.3 us (5%)
  matrix products  14.7 us (5%)
  local copies, waits for them, and re-layouts  14.1 us (5%)
  starting transfers between devices  13.9 us (5%)
  other arithmetic  7.77 us (3%)
    reduce_scatter x2, waiting for transfers between devices, scatter_axes(): nearer = lax.psum_scatter(array, axes[0], scatter_dimension=dim, tiled=True)  82.6 us
    all_to_all x1, waiting for transfers between devices, summed_rows(): return jnp.sum(lax.all_to_all(own, far, 0, 0, tiled=True), axis=0)  42.7 us
    all_to_all x2, blocking collectives, sent_to_all(): return lax.all_to_all(copies, axis, split_axis=0, concat_axis=0, tiled=True)  40.7 us
    psum x5, blocking collectives, one_axis_at_a_time(): return functools.reduce(lax.psum, axes, array)  39.3 us
    all_to_all x1, waiting for transfers between devices, sent_to_all(): return lax.all_to_all(copies, axis, split_axis=0, concat_axis=0, tiled=True)  21.9 us
    all_to_all x1, blocking collectives, sent_and_summed(): lax.all_to_all(in_blocks(array, dim, count), axis, 0, 0, tiled=True)  9.19 us
    all_to_all x1, starting transfers between devices, summed_rows(): return jnp.sum(lax.all_to_all(own, far, 0, 0, tiled=True), axis=0)  8.03 us
    dot_general x1, matrix products, token_product(): lax.dot_general(projected_rows, grad_rows, (((0,), (0,)), ((), ())), pref...  7.71 us
  transfers between devices with their start and end apart: 5, of which 5 were waited for; matrix products, arithmetic and copies ran while one was open for 1% of the time, Pallas kernels for 0%

commit v1 on v0

v1 whole, which is shorter than its diff:
```python
import functools

import jax
import jax.numpy as jnp
from jax import lax
from jax.experimental import pallas as pl
from jax.experimental.pallas import tpu as pltpu
from jax.sharding import Mesh
from jax.sharding import PartitionSpec as P

MESH = pl.DeviceIdType.MESH
TOKENS = 2048
FEATS = 512
R = 512
COLS = 1792
FF = 14336
BLOCKS = 4
RANKS = R // BLOCKS
PIECE = 128
ROWS = 16
TILE = 256
OFFSETS = (('project', 0), ('chain', 1), ('second', 5), ('third', 8), ('fourth', 12), ('forward', 13), ('multiply', 16), ('along_z', 19), ('along_x', 27))
PERIOD = 3
CHAINED = ()
FORWARDED = ()
SIZES = {"z": 8, "xl": 2, "c": 2, "y": 4, "xh": 2}
FAR_FIRST = (4, 3, 5, 2, 6, 1, 7)

first_fix = 0.9999734386011124
second_fix = 0.994079470779666


def f32(x):
    return x.astype(jnp.float32)


def bf16(x):
    return x.astype(jnp.bfloat16)


class Copies:
    def __init__(self, send_sems, recv_sems):
        self.send_sems, self.recv_sems, self.count = send_sems, recv_sems, 0

    def next(self):
        self.count += 1
        return self.count - 1

    def make(self, src, dst, recv=None, **device):
        k = self.next()
        return pltpu.make_async_remote_copy(
            src_ref=src,
            dst_ref=dst,
            send_sem=self.send_sems.at[k],
            recv_sem=self.recv_sems.at[k if recv is None else recv],
            device_id=device,
            device_id_type=MESH,
        )


def kernel(
    acts_h, grad_h, proj_h, weight_h, m1_h, m2_h,
    w_o, m1_o, m2_o,
    acts, grad, proj, proj_t, weight, m1, m2,
    s1, q1, r1, x1s, x1r, s2, r2, y2s, y2r, full,
    mine, core_s, core_r, z_s, z_own, z_r, x_s, x_r,
    sq, sq_z, sq_s, sq_c, upd, basis, new_w, new_m1, new_m2,
    send_sems, recv_sems, local_sems,
):
    z, xl, c = lax.axis_index("z"), lax.axis_index("xl"), lax.axis_index("c")
    y, xh = lax.axis_index("y"), lax.axis_index("xh")
    shard = y * 2 + xh
    me = {"z": z, "xl": xl, "c": c, "y": y, "xh": xh}

    def at(axis, step):
        return lax.rem(me[axis] + step, SIZES[axis])

    def shard_at(step):
        other = lax.rem(shard + step, 8)
        return {"y": lax.div(other, 2), "xh": lax.rem(other, 2)}

    loads = {}
    for k, (name, src, dst) in enumerate(
        (
            ("proj", proj_h, proj),
            ("acts", acts_h, acts),
            ("grad", grad_h, grad),
            ("m1", m1_h, m1),
            ("m2", m2_h, m2),
            ("weight", weight_h, weight),
        )
    ):
        loads[name] = pltpu.make_async_copy(src, dst, local_sems.at[k])
    loads["proj"].start()
    loads["acts"].start()

    partners = [{"z": at("z", d)} for d in range(1, 8)]
    partners += [shard_at(d) for d in range(1, 8)]
    partners += [{"c": 1 - c}, {"xl": 1 - xl}]
    barrier = pltpu.get_barrier_semaphore()
    for partner in partners:
        pl.semaphore_signal(barrier, inc=1, device_id=partner, device_id_type=MESH)

    loads["proj"].wait()
    proj_t[...] = proj[...].T
    loads["acts"].wait()
    for name in ("grad", "m1", "m2", "weight"):
        loads[name].start()

    copies = Copies(send_sems, recv_sems)
    sent = []

    def start(copy):
        copy.start()
        sent.append(copy)
        return copy

    def ranks_of(b):
        return jnp.concatenate(
            [proj_t[pl.ds(64 * k + ROWS * b, ROWS), :] for k in range(8)], axis=0
        )

    def project(lhs, token, count):
        rows = acts[pl.ds(pl.multiple_of(token, PIECE), count), :]
        return bf16(
            lax.dot_general(
                lhs, rows, (((1,), (1,)), ((), ())), preferred_element_type=jnp.float32
            )
        )

    st = [dict() for _ in range(BLOCKS)]

    def stage1(b):
        lhs = ranks_of(b)

        def x_half(h):
            token = 1024 + lax.rem(xh + h, 2) * 512
            out = project(lhs, token, 512)
            for k in range(4):
                s2[b, h, k] = out[:, k * PIECE : (k + 1) * PIECE]

        def y_quarter(d):
            out = project(lhs, at("y", d) * 256, 256)
            for k in range(2):
                s1[b, d, k] = out[:, k * PIECE : (k + 1) * PIECE]

        x_half(1)
        if b == 0:
            pl.semaphore_wait(barrier, len(partners))
        st[b]["r2"] = start(copies.make(s2.at[b, 1], r2.at[b], xh=1 - xh))
        y_quarter(2)
        if b in CHAINED:
            st[b]["q1"] = [
                start(copies.make(s1.at[b, 2, k], q1.at[b, k], y=at("y", d)))
                for k, d in enumerate((1, 3))
            ]
            y_quarter(1)
            y_quarter(3)
        else:
            st[b]["r1"] = [start(copies.make(s1.at[b, 2], r1.at[b, 2], y=at("y", 2)))]
            for k, d in enumerate((1, 3)):
                y_quarter(d)
                st[b]["r1"].append(
                    start(copies.make(s1.at[b, d], r1.at[b, k], y=at("y", d)))
                )
        x_half(0)
        y_quarter(0)

    def chain(b):
        if b not in CHAINED:
            return
        st[b]["r1"] = []
        for k, d in enumerate((1, 3)):
            st[b]["q1"][k].wait_recv()
            s1[b, d, k] = bf16(f32(s1[b, d, k]) + f32(q1[b, k]))
            st[b]["r1"].append(
                start(copies.make(s1.at[b, d], r1.at[b, k], y=at("y", d)))
            )

    def sum1(b, half):
        value = f32(s1[b, 0, half]) + f32(r1[b, 0, half]) + f32(r1[b, 1, half])
        return value if b in CHAINED else value + f32(r1[b, 2, half])

    def stage2(b):
        for copy in st[b]["r1"]:
            copy.wait_recv()
        x1s[b] = bf16(sum1(b, 1 - xh))
        st[b]["x1"] = start(copies.make(x1s.at[b], x1r.at[b], xh=1 - xh))
        st[b]["r2"].wait_recv()
        st[b]["y2"] = []
        for d in (2, 1, 3):
            other = at("y", d)
            y2s[b, d - 1] = bf16(f32(s2[b, 0, other]) + f32(r2[b, other]))
            st[b]["y2"].append(
                start(copies.make(y2s.at[b, d - 1], y2r.at[b, d - 1], y=other))
            )

    def stage3(b):
        st[b]["x1"].wait_recv()
        slot = 8 * b + y * 2 + xh
        full[0, slot] = bf16(sum1(b, xh) + f32(x1r[b]))
        st[b]["x3"] = start(copies.make(full.at[0, slot], full.at[0, slot], xh=1 - xh))
        for copy in st[b]["y2"]:
            copy.wait_recv()
        value = f32(s2[b, 0, y]) + f32(r2[b, y])
        for k in range(3):
            value += f32(y2r[b, k])
        slot = 8 * b + xh * 4 + y
        full[1, slot] = bf16(value)
        st[b]["y3"] = [
            start(copies.make(full.at[1, slot], full.at[1, slot], y=at("y", d)))
            for d in (2, 1, 3)
        ]

    def stage4(b):
        st[b]["x3"].wait_recv()
        pair = full.at[0, pl.ds(8 * b + y * 2, 2)]
        steps = (1, 3) if b in FORWARDED else (1, 3, 2)
        st[b]["y4"] = [start(copies.make(pair, pair, y=at("y", d))) for d in steps]
        for copy in st[b]["y3"]:
            copy.wait_recv()
        four = full.at[1, pl.ds(8 * b + xh * 4, 4)]
        st[b]["x4"] = start(copies.make(four, four, xh=1 - xh))

    def forward(b):
        if b not in FORWARDED:
            st[b]["y5"] = st[b]["y4"]
            return
        st[b]["y5"] = []
        for k, d in enumerate((1, 3)):
            st[b]["y4"][k].wait_recv()
            one = full.at[0, 8 * b + at("y", 4 - d) * 2 + k]
            st[b]["y5"].append(start(copies.make(one, one, y=at("y", d))))

    def parts(b):
        return ((0, 4), (4, 7)) if b == BLOCKS - 1 else ((0, 7),)

    def multiply(b):
        for copy in st[b]["y5"]:
            copy.wait_recv()
        st[b]["x4"].wait_recv()
        if b == 0:
            loads["grad"].wait()
        near = c == b % 2
        st[b]["near"] = near
        st[b]["core"] = []

        def columns(n, carry):
            here = pl.ds(pl.multiple_of(n * TILE, TILE), TILE)
            lhs = jnp.concatenate(
                [full[part, 8 * b + k] for part in range(2) for k in range(8)], axis=1
            )
            out = jnp.dot(lhs, grad[:, here], preferred_element_type=jnp.float32)

            @pl.when(near)
            def _():
                mine[b // 2, :, here] = out

            @pl.when(jnp.logical_not(near))
            def _():
                for k in range(8):
                    core_s[b, k, :, here] = bf16(out[k * ROWS : (k + 1) * ROWS])

            return carry

        for low, high in parts(b):
            span = pl.ds(low * TILE, (high - low) * TILE)
            copy = copies.make(core_s.at[b, :, :, span], core_r.at[b, :, :, span], c=1 - c)
            st[b]["core"].append(copy)
            lax.fori_loop(low, high, columns, 0)
            pl.when(jnp.logical_not(near))(copy.start)

    def along_z(b):
        j = b // 2
        st[b]["z"] = []
        for low, high in parts(b):
            span = pl.ds(low * TILE, (high - low) * TILE)
            st[b]["z"].append(
                [
                    copies.make(
                        z_s.at[j, at("z", d), :, span], z_r.at[j, d - 1, :, span], z=at("z", d)
                    )
                    for d in FAR_FIRST
                ]
            )

        @pl.when(st[b]["near"])
        def _():
            for (low, high), core, group in zip(parts(b), st[b]["core"], st[b]["z"]):
                span = slice(low * TILE, high * TILE)
                core.wait_recv()
                for k in range(8):
                    z_s[j, k, :, span] = bf16(
                        mine[j, k * ROWS : (k + 1) * ROWS, span] + f32(core_r[b, k, :, span])
                    )
                for copy in group:
                    copy.start()
                own = pl.ds(pl.multiple_of(z * ROWS, ROWS), ROWS)
                z_own[j, :, span] = mine[j, own, span] + f32(core_r[b, z, :, span])

    def along_x(b):
        j = b // 2
        spans = [pl.ds(low * TILE, (high - low) * TILE) for low, high in parts(b)]
        st[b]["x"] = [
            copies.make(x_s.at[j, :, span], x_r.at[j, :, span], xl=1 - xl) for span in spans
        ]

        @pl.when(st[b]["near"])
        def _():
            for (low, high), group, copy in zip(parts(b), st[b]["z"], st[b]["x"]):
                span = slice(low * TILE, high * TILE)
                for arrived in group:
                    arrived.wait_recv()
                value = z_own[j, :, span]
                for k in range(7):
                    value += f32(z_r[j, k, :, span])
                z_own[j, :, span] = value
                x_s[j, :, span] = bf16(value)
                copy.start()

    offset = pl.multiple_of((xl * 2 + c) * PIECE, PIECE)
    rows = proj.at[pl.ds(offset, PIECE)]
    basis_sem = copies.next()
    to_basis = [copies.make(rows, basis, recv=basis_sem, **shard_at(d)) for d in range(1, 8)]

    def send_basis():
        @pl.when(shard == z)
        def _():
            for copy in to_basis:
                copy.start()
            basis[...] = proj[pl.ds(offset, PIECE), :]

    stages = {
        "project": stage1, "chain": chain, "second": stage2, "third": stage3, "fourth": stage4,
        "forward": forward, "multiply": multiply, "along_z": along_z, "along_x": along_x,
    }
    order = sorted(
        (b * PERIOD + offset, b, name) for b in range(BLOCKS) for name, offset in OFFSETS
    )
    for _, b, name in order:
        stages[name](b)
        if (name, b) == ("multiply", BLOCKS - 1):
            send_basis()

    for b in range(BLOCKS):

        @pl.when(st[b]["near"])
        def _():
            for copy in st[b]["x"]:
                copy.wait_recv()

    value = jnp.zeros((8, 128), jnp.float32)
    for j in range(2):
        gradient = z_own[j] + f32(x_r[j])
        z_own[j] = gradient
        square = gradient * gradient
        square = square[:8] + square[8:]
        for k in range(COLS // 128):
            value += square[:, k * 128 : (k + 1) * 128]

    def exchange(value, step, slots, partners):
        sq[step] = value
        arriving = [
            start(copies.make(sq.at[step], slots.at[k], **partner))
            for k, partner in enumerate(partners)
        ]
        for k, copy in enumerate(arriving):
            copy.wait_recv()
            value += slots[k]
        return value

    value = exchange(value, 0, sq_c, [{"c": 1 - c}])
    value = exchange(value, 1, sq_s, [shard_at(d) for d in range(1, 8)])
    value = exchange(value, 2, sq_z, [{"z": at("z", d)} for d in FAR_FIRST])
    root_mean = jnp.sqrt(jnp.sum(value, keepdims=True) / (R * FF) + 1e-06)
    clip_factor = jnp.minimum(1.0, 4.0 / root_mean)

    for name in ("m1", "m2", "weight"):
        loads[name].wait()
    clipped = clip_factor * z_own[xl]
    moment1 = 0.9 * m1[...] + 0.1 * clipped
    moment2 = 0.95 * m2[...] + 0.05 * clipped * clipped
    upd[z, xl, c] = bf16(moment1 / first_fix / (jnp.sqrt(moment2 / second_fix) + 1e-08))

    def piece(zz, xx):
        return upd.at[zz, xx, c]

    across, last = {}, []

    def z_copy(part, step):
        return start(copies.make(part, part, z=at("z", step)))

    def pass_on(zz, key):
        across[key] = start(copies.make(piece(zz, xl), piece(zz, xl), xl=1 - xl))
        last.append(start(copies.make(piece(zz, xl), piece(zz, xl), c=1 - c)))

    def pass_core(zz, key):
        across[key].wait_recv()
        last.append(start(copies.make(piece(zz, 1 - xl), piece(zz, 1 - xl), c=1 - c)))

    coming = {step: z_copy(piece(z, xl), step) for step in (1, 7)}
    pass_on(z, 0)
    new_m1[...] = moment1
    new_m2[...] = moment2
    stores = [
        pltpu.make_async_copy(new_m1, m1_o, local_sems.at[6]),
        pltpu.make_async_copy(new_m2, m2_o, local_sems.at[7]),
    ]
    for store in stores:
        store.start()
    waiting = [(z, 0)]
    for hop in (1, 2, 3):
        arrived, coming = coming, {}
        for step in (1, 7):
            arrived[step].wait_recv()
            zz = at("z", hop * (8 - step))
            part = piece(zz, xl)
            if hop == 3:
                part = upd.at[zz, xl, c, :, pl.ds(0 if step == 1 else COLS // 2, COLS // 2)]
            coming[step] = z_copy(part, step)
            pass_on(zz, (hop, step))
            waiting.append((zz, (hop, step)))
        while len(waiting) > 2:
            pass_core(*waiting.pop(0))
    for step in (1, 7):
        coming[step].wait_recv()
    pass_on(at("z", 4), 4)
    waiting.append((at("z", 4), 4))
    for item in waiting:
        pass_core(*item)

    @pl.when(shard != z)
    def _():
        to_basis[0].wait_recv()

    for copy in last:
        copy.wait_recv()

    def out_columns(n, carry):
        here = pl.ds(pl.multiple_of(n * TILE, TILE), TILE)
        rows = jnp.concatenate(
            [upd[k // 4, (k // 2) % 2, k % 2, :, here] for k in range(32)], axis=0
        )
        change = jnp.dot(basis[...], rows, preferred_element_type=jnp.float32)
        new_w[:, here] = bf16(f32(weight[:, here]) - 0.2 * change)
        return carry

    lax.fori_loop(0, COLS // TILE, out_columns, 0)
    stores.append(pltpu.make_async_copy(new_w, w_o, local_sems.at[8]))
    stores[-1].start()

    assert copies.count <= SEMS
    for copy in sent:
        copy.wait_send()
    for b in range(BLOCKS):

        @pl.when(st[b]["near"])
        def _():
            for group in (*st[b]["z"], st[b]["x"]):
                for copy in group:
                    copy.wait_send()

        @pl.when(jnp.logical_not(st[b]["near"]))
        def _():
            for copy in st[b]["core"]:
                copy.wait_send()

    @pl.when(shard == z)
    def _():
        for copy in to_basis:
            copy.wait_send()

    for store in stores:
        store.wait()


def handed_on(w, m1, m2, w_o, m1_o, m2_o):
    w_o[...], m1_o[...], m2_o[...] = w[...], m1[...], m2[...]


SEMS = 224


def step(acts, grad_out, projector, weight, moment1, moment2):
    hbm = pl.BlockSpec(memory_space=pltpu.MemorySpace.HBM)
    half, full = jnp.bfloat16, jnp.float32
    pieces = (RANKS, PIECE)
    owned = (ROWS, COLS)
    scratch = [
        pltpu.VMEM(acts.shape, half),
        pltpu.VMEM(grad_out.shape, half),
        pltpu.VMEM(projector.shape, half),
        pltpu.VMEM(projector.shape, half),
        pltpu.VMEM(weight.shape, half),
        pltpu.VMEM(owned, full),
        pltpu.VMEM(owned, full),
        pltpu.VMEM((BLOCKS, 4, 2, *pieces), half),
        pltpu.VMEM((BLOCKS, 2, *pieces), half),
        pltpu.VMEM((BLOCKS, 3, 2, *pieces), half),
        pltpu.VMEM((BLOCKS, *pieces), half),
        pltpu.VMEM((BLOCKS, *pieces), half),
        pltpu.VMEM((BLOCKS, 2, 4, *pieces), half),
        pltpu.VMEM((BLOCKS, 4, *pieces), half),
        pltpu.VMEM((BLOCKS, 3, *pieces), half),
        pltpu.VMEM((BLOCKS, 3, *pieces), half),
        pltpu.VMEM((2, BLOCKS * 8, *pieces), half),
        pltpu.VMEM((2, RANKS, COLS), full),
        pltpu.VMEM((BLOCKS, 8, *owned), half),
        pltpu.VMEM((BLOCKS, 8, *owned), half),
        pltpu.VMEM((2, 8, *owned), half),
        pltpu.VMEM((2, *owned), full),
        pltpu.VMEM((2, 7, *owned), half),
        pltpu.VMEM((2, *owned), half),
        pltpu.VMEM((2, *owned), half),
        pltpu.VMEM((3, 8, 128), full),
        pltpu.VMEM((7, 8, 128), full),
        pltpu.VMEM((7, 8, 128), full),
        pltpu.VMEM((1, 8, 128), full),
        pltpu.VMEM((8, 2, 2, *owned), half),
        pltpu.VMEM((PIECE, R), half),
        pltpu.VMEM(weight.shape, half),
        pltpu.VMEM(owned, full),
        pltpu.VMEM(owned, full),
        pltpu.SemaphoreType.DMA((SEMS,)),
        pltpu.SemaphoreType.DMA((SEMS,)),
        pltpu.SemaphoreType.DMA((9,)),
    ]
    outs = (
        jax.ShapeDtypeStruct(weight.shape, half),
        jax.ShapeDtypeStruct(owned, full),
        jax.ShapeDtypeStruct(owned, full),
    )
    results = pl.pallas_call(
        kernel,
        out_shape=outs,
        in_specs=[hbm] * 6,
        out_specs=(hbm,) * 3,
        scratch_shapes=scratch,
        name="galore_step",
        compiler_params=pltpu.CompilerParams(
            collective_id=0, has_side_effects=True, vmem_limit_bytes=56 << 20
        ),
    )(acts, grad_out, projector, weight, moment1, moment2)
    return pl.pallas_call(
        handed_on,
        out_shape=outs,
        name="handed_on",
    )(*results)


def solution(mesh):
    finer = Mesh(mesh.devices.reshape(8, 2, 2, 4, 2), ("z", "xl", "c", "y", "xh"))
    dp, shard = ("z", "xl", "c"), ("y", "xh")
    both = P(dp, shard)
    return jax.shard_map(
        step,
        mesh=finer,
        in_specs=(both, both, P(shard, None), both, both, both),
        out_specs=(both, both, both),
        check_vma=False,
    )
```

time: 306 us -> 102 us (0.33)
  waiting for transfers between devices: 149 us -> 0 us
  Pallas kernels: 0 us -> 101 us
  blocking collectives: 89.1 us -> 0 us
  between operations: 16.3 us -> 0.64 us
  matrix products: 14.7 us -> 0 us
  local copies, waits for them, and re-layouts: 14.1 us -> 0 us
  starting transfers between devices: 13.9 us -> 0 us
  other arithmetic: 7.77 us -> 0 us
    pallas_call x0 -> x2, Pallas kernels: none -> 101 us  [the longest x1 99.5 us: step(): pl.pallas_call(kernel, out_shape=outs, in_specs=[hbm] * 6, out_specs=(hbm...]
    reduce_scatter x2 -> x0, waiting for transfers between devices: 82.6 us -> none  [scatter_axes(): nearer = lax.psum_scatter(array, axes[0], scatter_dimension=dim, tiled=True)]
    all_to_all x2 -> x0, waiting for transfers between devices: 64.6 us -> none  [the longest x1 42.7 us: summed_rows(): return jnp.sum(lax.all_to_all(own, far, 0, 0, tiled=True), axis=0)]
    all_to_all x3 -> x0, blocking collectives: 49.9 us -> none  [the longest x2 40.7 us: sent_to_all(): return lax.all_to_all(copies, axis, split_axis=0, concat_axis=0, tiled=True)]
    psum x5 -> x0, blocking collectives: 39.3 us -> none  [one_axis_at_a_time(): return functools.reduce(lax.psum, axes, array)]
    dot_general x3 -> x0, matrix products: 14.7 us -> none  [the longest x1 7.71 us: token_product(): lax.dot_general(projected_rows, grad_rows, (((0,), (0,)), ((), ())), pref...]
    all_to_all x2 -> x0, starting transfers between devices: 13.8 us -> none  [the longest x1 8.03 us: summed_rows(): return jnp.sum(lax.all_to_all(own, far, 0, 0, tiled=True), axis=0)]
    reduce_sum x3 -> x0, other arithmetic: 5.94 us -> none  [the longest x1 3.72 us: sent_and_summed(): return jnp.sum(pieces, axis=0)]
  transfers between devices with their start and end apart: 5 -> 0, of which waited for: 5 -> 0; matrix products, arithmetic and copies ran while one was open for 1% -> 0% of each run, Pallas kernels for 0% -> 0%
where the time goes in v1:
time: 102 us
  Pallas kernels  101 us (99%)
    pallas_call x1, Pallas kernels, step(): pl.pallas_call(kernel, out_shape=outs, in_specs=[hbm] * 6, out_specs=(hbm...  99.5 us

profile of v1, /device:TPU:1, one launch (start us, length us, event | category | flops | bytes accessed | tf_op | source)
XLA Modules:
  0.0 102.1 jit_solution(1146460473796339566)
XLA Ops:
  0.6 99.5 %galore_step.1 = (bf16[128,1792]{1,0:T(8,128)(2,1)}, f32[16,1792]{1,0:T(8,128)}, f32[16,1792]{1,0:T(8,128)}) custom-call(bf16[2048,512]{1,0:T(8,128)(2,1)} %acts_h.1, bf16[2048,1792]{1,0:T(8,128)(2,1)} %grad_h.1, bf16[512,512]{1,0:T(8,128)(2,1)} %proj_h.1, bf16[128,1792]{1,0:T(8,128)(2,1)} %weight_h.1, f32[16,1792]{1,0:T(8,128)} %m1_h.1, f32[16,1792]{1,0:T(8,128)} %m2_h.1), custom_call_target="tpu_custom_call" | custom-call | tf_op jit(solution)/shard_map/galore_step/pallas_call | solution.py:533
  100.1 1.9 %handed_on.1 = (bf16[128,1792]{1,0:T(8,128)(2,1)}, f32[16,1792]{1,0:T(8,128)}, f32[16,1792]{1,0:T(8,128)}) custom-call(bf16[128,1792]{1,0:T(8,128)(2,1)} %get-tuple-element.6.w, f32[16,1792]{1,0:T(8,128)} %get-tuple-element.7.m1, f32[16,1792]{1,0:T(8,128)} %get-tuple-element.8.m2), custom_call_target="tpu_custom_call" | custom-call | tf_op jit(solution)/shard_map/handed_on/pallas_call | solution.py:544

commit v2 on v1

--- a/solution.py
+++ b/solution.py
@@ -18,11 +18,16 @@
 RANKS = R // BLOCKS
 PIECE = 128
 ROWS = 16
-TILE = 256
-OFFSETS = (('project', 0), ('chain', 1), ('second', 5), ('third', 8), ('fourth', 12), ('forward', 13), ('multiply', 16), ('along_z', 19), ('along_x', 27))
+TILE = 896
+OFFSETS = dict(p=0, sx=5, sy=4.9, tx=8, ty=7.9, fy=12, fx=11.9, m=16, n=16.1, o=16.2, z=19, x=27)
 PERIOD = 3
-CHAINED = ()
-FORWARDED = ()
+ORDER = [
+    (name, b)
+    for _, b, name in sorted(
+        (b * PERIOD + offset, b, name) for b in range(BLOCKS) for name, offset in OFFSETS.items()
+    )
+]
+FIRST_PRODUCT = next(item for item in ORDER if item[0] == "m")
 SIZES = {"z": 8, "xl": 2, "c": 2, "y": 4, "xh": 2}
 FAR_FIRST = (4, 3, 5, 2, 6, 1, 7)
 
@@ -62,9 +67,9 @@
     acts_h, grad_h, proj_h, weight_h, m1_h, m2_h,
     w_o, m1_o, m2_o,
     acts, grad, proj, proj_t, weight, m1, m2,
-    s1, q1, r1, x1s, x1r, s2, r2, y2s, y2r, full,
+    s1, r1, x1s, x1r, s2, r2, y2s, y2r, full,
     mine, core_s, core_r, z_s, z_own, z_r, x_s, x_r,
-    sq, sq_z, sq_s, sq_c, upd, basis, new_w, new_m1, new_m2,
+    sq, sq_z, sq_s, sq_c, upd, basis,
     send_sems, recv_sems, local_sems,
 ):
     z, xl, c = lax.axis_index("z"), lax.axis_index("xl"), lax.axis_index("c")
@@ -130,7 +135,7 @@
 
     st = [dict() for _ in range(BLOCKS)]
 
-    def stage1(b):
+    def project_block(b):
         lhs = ranks_of(b)
 
         def x_half(h):
@@ -145,47 +150,30 @@
                 s1[b, d, k] = out[:, k * PIECE : (k + 1) * PIECE]
 
         x_half(1)
-        if b == 0:
+        if b == ORDER[0][1]:
             pl.semaphore_wait(barrier, len(partners))
         st[b]["r2"] = start(copies.make(s2.at[b, 1], r2.at[b], xh=1 - xh))
         y_quarter(2)
-        if b in CHAINED:
-            st[b]["q1"] = [
-                start(copies.make(s1.at[b, 2, k], q1.at[b, k], y=at("y", d)))
-                for k, d in enumerate((1, 3))
-            ]
-            y_quarter(1)
-            y_quarter(3)
-        else:
-            st[b]["r1"] = [start(copies.make(s1.at[b, 2], r1.at[b, 2], y=at("y", 2)))]
-            for k, d in enumerate((1, 3)):
-                y_quarter(d)
-                st[b]["r1"].append(
-                    start(copies.make(s1.at[b, d], r1.at[b, k], y=at("y", d)))
-                )
+        st[b]["r1"] = [start(copies.make(s1.at[b, 2], r1.at[b, 2], y=at("y", 2)))]
+        for k, d in enumerate((1, 3)):
+            y_quarter(d)
+            st[b]["r1"].append(start(copies.make(s1.at[b, d], r1.at[b, k], y=at("y", d))))
         x_half(0)
         y_quarter(0)
 
-    def chain(b):
-        if b not in CHAINED:
-            return
-        st[b]["r1"] = []
-        for k, d in enumerate((1, 3)):
-            st[b]["q1"][k].wait_recv()
-            s1[b, d, k] = bf16(f32(s1[b, d, k]) + f32(q1[b, k]))
-            st[b]["r1"].append(
-                start(copies.make(s1.at[b, d], r1.at[b, k], y=at("y", d)))
-            )
-
     def sum1(b, half):
-        value = f32(s1[b, 0, half]) + f32(r1[b, 0, half]) + f32(r1[b, 1, half])
-        return value if b in CHAINED else value + f32(r1[b, 2, half])
-
-    def stage2(b):
+        value = f32(s1[b, 0, half])
+        for k in range(3):
+            value += f32(r1[b, k, half])
+        return value
+
+    def second_x(b):
         for copy in st[b]["r1"]:
             copy.wait_recv()
         x1s[b] = bf16(sum1(b, 1 - xh))
         st[b]["x1"] = start(copies.make(x1s.at[b], x1r.at[b], xh=1 - xh))
+
+    def second_y(b):
         st[b]["r2"].wait_recv()
         st[b]["y2"] = []
         for d in (2, 1, 3):
@@ -195,11 +183,13 @@
                 start(copies.make(y2s.at[b, d - 1], y2r.at[b, d - 1], y=other))
             )
 
-    def stage3(b):
+    def third_x(b):
         st[b]["x1"].wait_recv()
         slot = 8 * b + y * 2 + xh
         full[0, slot] = bf16(sum1(b, xh) + f32(x1r[b]))
         st[b]["x3"] = start(copies.make(full.at[0, slot], full.at[0, slot], xh=1 - xh))
+
+    def third_y(b):
         for copy in st[b]["y2"]:
             copy.wait_recv()
         value = f32(s2[b, 0, y]) + f32(r2[b, y])
@@ -212,38 +202,37 @@
             for d in (2, 1, 3)
         ]
 
-    def stage4(b):
+    def fourth_y(b):
         st[b]["x3"].wait_recv()
         pair = full.at[0, pl.ds(8 * b + y * 2, 2)]
-        steps = (1, 3) if b in FORWARDED else (1, 3, 2)
-        st[b]["y4"] = [start(copies.make(pair, pair, y=at("y", d))) for d in steps]
+        st[b]["y4"] = [start(copies.make(pair, pair, y=at("y", d))) for d in (1, 3, 2)]
+
+    def fourth_x(b):
         for copy in st[b]["y3"]:
             copy.wait_recv()
         four = full.at[1, pl.ds(8 * b + xh * 4, 4)]
         st[b]["x4"] = start(copies.make(four, four, xh=1 - xh))
 
-    def forward(b):
-        if b not in FORWARDED:
-            st[b]["y5"] = st[b]["y4"]
-            return
-        st[b]["y5"] = []
-        for k, d in enumerate((1, 3)):
-            st[b]["y4"][k].wait_recv()
-            one = full.at[0, 8 * b + at("y", 4 - d) * 2 + k]
-            st[b]["y5"].append(start(copies.make(one, one, y=at("y", d))))
-
     def parts(b):
-        return ((0, 4), (4, 7)) if b == BLOCKS - 1 else ((0, 7),)
-
-    def multiply(b):
-        for copy in st[b]["y5"]:
+        return ((0, 1), (1, 2)) if b == BLOCKS - 1 else ((0, 2),)
+
+    def span_of(part):
+        return pl.ds(part[0] * TILE, (part[1] - part[0]) * TILE)
+
+    def arrived(b):
+        for copy in st[b]["y4"]:
             copy.wait_recv()
         st[b]["x4"].wait_recv()
-        if b == 0:
-            loads["grad"].wait()
-        near = c == b % 2
-        st[b]["near"] = near
+        st[b]["near"] = c == b % 2
         st[b]["core"] = []
+        for part in parts(b):
+            span = span_of(part)
+            st[b]["core"].append(
+                copies.make(core_s.at[b, :, :, span], core_r.at[b, :, :, span], c=1 - c)
+            )
+
+    def multiply(b, low, high):
+        near = st[b]["near"]
 
         def columns(n, carry):
             here = pl.ds(pl.multiple_of(n * TILE, TILE), TILE)
@@ -263,18 +252,26 @@
 
             return carry
 
-        for low, high in parts(b):
-            span = pl.ds(low * TILE, (high - low) * TILE)
-            copy = copies.make(core_s.at[b, :, :, span], core_r.at[b, :, :, span], c=1 - c)
-            st[b]["core"].append(copy)
-            lax.fori_loop(low, high, columns, 0)
-            pl.when(jnp.logical_not(near))(copy.start)
+        lax.fori_loop(low, high, columns, 0)
+
+    def multiply_0(b):
+        arrived(b)
+        pass
+
+    def multiply_1(b):
+        multiply(b, 0, 1)
+        if len(parts(b)) > 1:
+            pl.when(jnp.logical_not(st[b]["near"]))(st[b]["core"][0].start)
+
+    def multiply_2(b):
+        multiply(b, 1, 2)
+        pl.when(jnp.logical_not(st[b]["near"]))(st[b]["core"][-1].start)
 
     def along_z(b):
         j = b // 2
         st[b]["z"] = []
-        for low, high in parts(b):
-            span = pl.ds(low * TILE, (high - low) * TILE)
+        for part in parts(b):
+            span = span_of(part)
             st[b]["z"].append(
                 [
                     copies.make(
@@ -300,7 +297,7 @@
 
     def along_x(b):
         j = b // 2
-        spans = [pl.ds(low * TILE, (high - low) * TILE) for low, high in parts(b)]
+        spans = [span_of(part) for part in parts(b)]
         st[b]["x"] = [
             copies.make(x_s.at[j, :, span], x_r.at[j, :, span], xl=1 - xl) for span in spans
         ]
@@ -331,15 +328,15 @@
             basis[...] = proj[pl.ds(offset, PIECE), :]
 
     stages = {
-        "project": stage1, "chain": chain, "second": stage2, "third": stage3, "fourth": stage4,
-        "forward": forward, "multiply": multiply, "along_z": along_z, "along_x": along_x,
+        "p": project_block, "sx": second_x, "sy": second_y, "tx": third_x, "ty": third_y,
+        "fy": fourth_y, "fx": fourth_x, "m": multiply_0, "n": multiply_1, "o": multiply_2,
+        "z": along_z, "x": along_x,
     }
-    order = sorted(
-        (b * PERIOD + offset, b, name) for b in range(BLOCKS) for name, offset in OFFSETS
-    )
-    for _, b, name in order:
+    for name, b in ORDER:
+        if (name, b) == FIRST_PRODUCT:
+            loads["grad"].wait()
         stages[name](b)
-        if (name, b) == ("multiply", BLOCKS - 1):
+        if (name, b) == ("o", BLOCKS - 1):
             send_basis()
 
     for b in range(BLOCKS):
@@ -385,49 +382,49 @@
     def piece(zz, xx):
         return upd.at[zz, xx, c]
 
-    across, last = {}, []
+    across, last = [], []
 
     def z_copy(part, step):
         return start(copies.make(part, part, z=at("z", step)))
 
-    def pass_on(zz, key):
-        across[key] = start(copies.make(piece(zz, xl), piece(zz, xl), xl=1 - xl))
-        last.append(start(copies.make(piece(zz, xl), piece(zz, xl), c=1 - c)))
-
-    def pass_core(zz, key):
-        across[key].wait_recv()
-        last.append(start(copies.make(piece(zz, 1 - xl), piece(zz, 1 - xl), c=1 - c)))
-
-    coming = {step: z_copy(piece(z, xl), step) for step in (1, 7)}
-    pass_on(z, 0)
-    new_m1[...] = moment1
-    new_m2[...] = moment2
-    stores = [
-        pltpu.make_async_copy(new_m1, m1_o, local_sems.at[6]),
-        pltpu.make_async_copy(new_m2, m2_o, local_sems.at[7]),
-    ]
-    for store in stores:
-        store.start()
-    waiting = [(z, 0)]
+    halves = [pl.ds(k * (COLS // 2), COLS // 2) for k in range(2)]
+
+    def pass_on(step, k=None):
+        zz = at("z", step)
+        span = slice(None) if k is None else halves[k]
+        part = upd.at[zz, xl, c, :, span]
+        other = upd.at[zz, 1 - xl, c, :, span]
+        across.append((start(copies.make(part, part, xl=1 - xl)), other))
+        last.append(start(copies.make(part, part, c=1 - c)))
+
+    def pass_core(keep):
+        while len(across) > keep:
+            copy, other = across.pop(0)
+            copy.wait_recv()
+            last.append(start(copies.make(other, other, c=1 - c)))
+
+    coming = {}
+    for k in range(2):
+        for step in (1, 7):
+            coming[step, k] = z_copy(upd.at[z, xl, c, :, halves[k]], step)
+    opposite = z_copy(piece(z, xl), 4)
+    pass_on(0)
+    m1_o[...] = moment1
+    m2_o[...] = moment2
     for hop in (1, 2, 3):
         arrived, coming = coming, {}
-        for step in (1, 7):
-            arrived[step].wait_recv()
-            zz = at("z", hop * (8 - step))
-            part = piece(zz, xl)
-            if hop == 3:
-                part = upd.at[zz, xl, c, :, pl.ds(0 if step == 1 else COLS // 2, COLS // 2)]
-            coming[step] = z_copy(part, step)
-            pass_on(zz, (hop, step))
-            waiting.append((zz, (hop, step)))
-        while len(waiting) > 2:
-            pass_core(*waiting.pop(0))
-    for step in (1, 7):
-        coming[step].wait_recv()
-    pass_on(at("z", 4), 4)
-    waiting.append((at("z", 4), 4))
-    for item in waiting:
-        pass_core(*item)
+        if hop == 3:
+            opposite.wait_recv()
+            pass_on(4)
+        for k in range(2):
+            for step in (1, 7):
+                arrived[step, k].wait_recv()
+                zz = at("z", hop * (8 - step))
+                if hop < 3:
+                    coming[step, k] = z_copy(upd.at[zz, xl, c, :, halves[k]], step)
+                pass_on(hop * (8 - step), k)
+        pass_core(4)
+    pass_core(0)
 
     @pl.when(shard != z)
     def _():
@@ -442,13 +439,10 @@
             [upd[k // 4, (k // 2) % 2, k % 2, :, here] for k in range(32)], axis=0
         )
         change = jnp.dot(basis[...], rows, preferred_element_type=jnp.float32)
-        new_w[:, here] = bf16(f32(weight[:, here]) - 0.2 * change)
+        w_o[:, here] = bf16(f32(weight[:, here]) - 0.2 * change)
         return carry
 
     lax.fori_loop(0, COLS // TILE, out_columns, 0)
-    stores.append(pltpu.make_async_copy(new_w, w_o, local_sems.at[8]))
-    stores[-1].start()
-
     assert copies.count <= SEMS
     for copy in sent:
         copy.wait_send()
@@ -470,15 +464,8 @@
         for copy in to_basis:
             copy.wait_send()
 
-    for store in stores:
-        store.wait()
-
-
-def handed_on(w, m1, m2, w_o, m1_o, m2_o):
-    w_o[...], m1_o[...], m2_o[...] = w[...], m1[...], m2[...]
-
-
-SEMS = 224
+
+SEMS = 256
 
 
 def step(acts, grad_out, projector, weight, moment1, moment2):
@@ -495,7 +482,6 @@
         pltpu.VMEM(owned, full),
         pltpu.VMEM(owned, full),
         pltpu.VMEM((BLOCKS, 4, 2, *pieces), half),
-        pltpu.VMEM((BLOCKS, 2, *pieces), half),
         pltpu.VMEM((BLOCKS, 3, 2, *pieces), half),
         pltpu.VMEM((BLOCKS, *pieces), half),
         pltpu.VMEM((BLOCKS, *pieces), half),
@@ -518,9 +504,6 @@
         pltpu.VMEM((1, 8, 128), full),
         pltpu.VMEM((8, 2, 2, *owned), half),
         pltpu.VMEM((PIECE, R), half),
-        pltpu.VMEM(weight.shape, half),
-        pltpu.VMEM(owned, full),
-        pltpu.VMEM(owned, full),
         pltpu.SemaphoreType.DMA((SEMS,)),
         pltpu.SemaphoreType.DMA((SEMS,)),
         pltpu.SemaphoreType.DMA((9,)),
@@ -532,20 +515,16 @@
     )
     results = pl.pallas_call(
         kernel,
-        out_shape=outs,
+        out_shape=tuple(pltpu.VMEM(out.shape, out.dtype) for out in outs),
         in_specs=[hbm] * 6,
-        out_specs=(hbm,) * 3,
+        out_specs=(pl.BlockSpec(memory_space=pltpu.MemorySpace.VMEM),) * 3,
         scratch_shapes=scratch,
         name="galore_step",
         compiler_params=pltpu.CompilerParams(
-            collective_id=0, has_side_effects=True, vmem_limit_bytes=56 << 20
+            collective_id=0, has_side_effects=True, vmem_limit_bytes=48 << 20
         ),
     )(acts, grad_out, projector, weight, moment1, moment2)
-    return pl.pallas_call(
-        handed_on,
-        out_shape=outs,
-        name="handed_on",
-    )(*results)
+    return results
 
 
 def solution(mesh):

time: 102 us -> 103 us (level)
  local copies, waits for them, and re-layouts: 0 us -> 7.5 us
  Pallas kernels: 101 us -> 94.9 us
    unnamed x0 -> x13, local copies, waits for them, and re-layouts: none -> 7.5 us
    pallas_call x2 -> x1, Pallas kernels: 101 us -> 94.9 us  [step(): pl.pallas_call(kernel, out_shape=tuple((pltpu.VMEM(out.shape, out.dtype)...]
where the time goes in v2:
time: 103 us
  Pallas kernels  94.9 us (92%)
  local copies, waits for them, and re-layouts  7.5 us (7%)
    pallas_call x1, Pallas kernels, step(): pl.pallas_call(kernel, out_shape=tuple((pltpu.VMEM(out.shape, out.dtype)...  94.9 us
    unnamed x13, local copies, waits for them, and re-layouts  7.5 us

profile of v2, /device:TPU:1, one launch (start us, length us, event | category | flops | bytes accessed | tf_op | source)
XLA Modules:
  0.0 103.1 jit_solution(6601304342222201118)
XLA Ops:
  0.6 0.0 copy-start
  0.6 1.6 %copy-done = bf16[2048,512]{1,0:T(8,128)(2,1)S(1)} copy-done((bf16[2048,512]{1,0:T(8,128)(2,1)S(1)}, bf16[2048,512]{1,0:T(8,128)(2,1)}, u32[]{:S(2)}) %copy-start) | copy-done | bytes 2097176
  2.2 0.0 copy-start.1
  2.2 1.0 %copy-done.1 = bf16[512,512]{1,0:T(8,128)(2,1)S(1)} copy-done((bf16[512,512]{1,0:T(8,128)(2,1)S(1)}, bf16[512,512]{1,0:T(8,128)(2,1)}, u32[]{:S(2)}) %copy-start.1) | copy-done | bytes 524312
  3.3 0.0 copy-start.2
  3.3 1.0 copy-done.2
  4.3 0.0 copy-start.3
  4.3 0.9 copy-done.3
  5.2 0.0 copy-start.4
  5.2 0.9 copy-done.4
  6.1 94.9 %galore_step.1 = (bf16[128,1792]{1,0:T(8,128)(2,1)S(1)}, f32[16,1792]{1,0:T(8,128)S(1)}, f32[16,1792]{1,0:T(8,128)S(1)}) custom-call(bf16[2048,512]{1,0:T(8,128)(2,1)S(1)} %copy-done, bf16[2048,1792]{1,0:T(8,128)(2,1)} %grad_h.1, bf16[512,512]{1,0:T(8,128)(2,1)S(1)} %copy-done.1, bf16[128,1792]{1,0:T(8,128)(2,1)S(1)} %copy-done.2, f32[16,1792]{1,0:T(8,128)S(1)} %copy-done.3, ...), custom_call_target="tpu_custom_call" | custom-call | tf_op jit(solution)/shard_map/galore_step/pallas_call | solution.py:516
  101.0 0.8 copy.12
  101.8 0.6 copy.13
  102.4 0.6 copy.14
Async XLA Ops:
  0.6 1.6 %copy-start = (bf16[2048,512]{1,0:T(8,128)(2,1)S(1)}, bf16[2048,512]{1,0:T(8,128)(2,1)}, u32[]{:S(2)}) copy-start(bf16[2048,512]{1,0:T(8,128)(2,1)} %acts_h.1) | copy-start | bytes 6291460
  2.2 1.0 %copy-start.1 = (bf16[512,512]{1,0:T(8,128)(2,1)S(1)}, bf16[512,512]{1,0:T(8,128)(2,1)}, u32[]{:S(2)}) copy-start(bf16[512,512]{1,0:T(8,128)(2,1)} %proj_h.1) | copy-start | bytes 1572868
  3.3 1.0 copy-start.2
  4.3 0.9 copy-start.3
  5.2 0.9 copy-start.4

commit v3 on v2

--- a/solution.py
+++ b/solution.py
@@ -521,7 +521,7 @@
         scratch_shapes=scratch,
         name="galore_step",
         compiler_params=pltpu.CompilerParams(
-            collective_id=0, has_side_effects=True, vmem_limit_bytes=48 << 20
+            collective_id=0, has_side_effects=True, vmem_limit_bytes=56 << 20
         ),
     )(acts, grad_out, projector, weight, moment1, moment2)
     return results

time: 103 us -> 97.9 us (0.950)
  local copies, waits for them, and re-layouts: 7.5 us -> 2.06 us
    unnamed x13 -> x3, local copies, waits for them, and re-layouts: 7.5 us -> 2.06 us
where the time goes in v3:
time: 97.9 us; the launch traced here: 97.8 us
  Pallas kernels  95.1 us (97%)
  local copies, waits for them, and re-layouts  2.06 us (2%)
    pallas_call x1, Pallas kernels, step(): pl.pallas_call(kernel, out_shape=tuple((pltpu.VMEM(out.shape, out.dtype)...  95.1 us
    unnamed x3, local copies, waits for them, and re-layouts  2.06 us

profile of v3, /device:TPU:1, one launch (start us, length us, event | category | flops | bytes accessed | tf_op | source)
XLA Modules:
  0.0 97.8 jit_solution(3858364976569170504)
XLA Ops:
  0.6 95.1 %galore_step.1 = (bf16[128,1792]{1,0:T(8,128)(2,1)S(1)}, f32[16,1792]{1,0:T(8,128)S(1)}, f32[16,1792]{1,0:T(8,128)S(1)}) custom-call(bf16[2048,512]{1,0:T(8,128)(2,1)} %acts_h.1, bf16[2048,1792]{1,0:T(8,128)(2,1)} %grad_h.1, bf16[512,512]{1,0:T(8,128)(2,1)} %proj_h.1, bf16[128,1792]{1,0:T(8,128)(2,1)} %weight_h.1, f32[16,1792]{1,0:T(8,128)} %m1_h.1, ...), custom_call_target="tpu_custom_call" | custom-call | tf_op jit(solution)/shard_map/galore_step/pallas_call | solution.py:516
  95.7 0.8 copy.12
  96.5 0.6 copy.13
  97.2 0.6 copy.14

commit v4 on v3

--- a/solution.py
+++ b/solution.py
@@ -69,7 +69,7 @@
     acts, grad, proj, proj_t, weight, m1, m2,
     s1, r1, x1s, x1r, s2, r2, y2s, y2r, full,
     mine, core_s, core_r, z_s, z_own, z_r, x_s, x_r,
-    sq, sq_z, sq_s, sq_c, upd, basis,
+    sq, sq_z, sq_s, upd, basis,
     send_sems, recv_sems, local_sems,
 ):
     z, xl, c = lax.axis_index("z"), lax.axis_index("xl"), lax.axis_index("c")
@@ -102,6 +102,9 @@
     partners = [{"z": at("z", d)} for d in range(1, 8)]
     partners += [shard_at(d) for d in range(1, 8)]
     partners += [{"c": 1 - c}, {"xl": 1 - xl}]
+    partners += [{"c": 1 - c, **shard_at(d)} for d in range(1, 8)]
+    nearby = [shard_at(d) for d in range(1, 8)]
+    nearby += [{"c": 1 - c, **device} for device in nearby] + [{"c": 1 - c}]
     barrier = pltpu.get_barrier_semaphore()
     for partner in partners:
         pl.semaphore_signal(barrier, inc=1, device_id=partner, device_id_type=MESH)
@@ -366,9 +369,8 @@
             value += slots[k]
         return value
 
-    value = exchange(value, 0, sq_c, [{"c": 1 - c}])
-    value = exchange(value, 1, sq_s, [shard_at(d) for d in range(1, 8)])
-    value = exchange(value, 2, sq_z, [{"z": at("z", d)} for d in FAR_FIRST])
+    value = exchange(value, 0, sq_s, nearby)
+    value = exchange(value, 1, sq_z, [{"z": at("z", d)} for d in FAR_FIRST])
     root_mean = jnp.sqrt(jnp.sum(value, keepdims=True) / (R * FF) + 1e-06)
     clip_factor = jnp.minimum(1.0, 4.0 / root_mean)
 
@@ -500,8 +502,7 @@
         pltpu.VMEM((2, *owned), half),
         pltpu.VMEM((3, 8, 128), full),
         pltpu.VMEM((7, 8, 128), full),
-        pltpu.VMEM((7, 8, 128), full),
-        pltpu.VMEM((1, 8, 128), full),
+        pltpu.VMEM((15, 8, 128), full),
         pltpu.VMEM((8, 2, 2, *owned), half),
         pltpu.VMEM((PIECE, R), half),
         pltpu.SemaphoreType.DMA((SEMS,)),

time: 97.9 us -> 97.4 us (level)
  no operation moved by 1% of the time
where the time goes in v4:
time: 97.4 us; the launch traced here: 97.3 us
  Pallas kernels  94.6 us (97%)
  local copies, waits for them, and re-layouts  2.06 us (2%)
    pallas_call x1, Pallas kernels, step(): pl.pallas_call(kernel, out_shape=tuple((pltpu.VMEM(out.shape, out.dtype)...  94.6 us
    unnamed x3, local copies, waits for them, and re-layouts  2.06 us

profile of v4, /device:TPU:1, one launch (start us, length us, event | category | flops | bytes accessed | tf_op | source)
XLA Modules:
  0.0 97.3 jit_solution(8129025193626591913)
XLA Ops:
  0.6 94.6 %galore_step.1 = (bf16[128,1792]{1,0:T(8,128)(2,1)S(1)}, f32[16,1792]{1,0:T(8,128)S(1)}, f32[16,1792]{1,0:T(8,128)S(1)}) custom-call(bf16[2048,512]{1,0:T(8,128)(2,1)} %acts_h.1, bf16[2048,1792]{1,0:T(8,128)(2,1)} %grad_h.1, bf16[512,512]{1,0:T(8,128)(2,1)} %proj_h.1, bf16[128,1792]{1,0:T(8,128)(2,1)} %weight_h.1, f32[16,1792]{1,0:T(8,128)} %m1_h.1, ...), custom_call_target="tpu_custom_call" | custom-call | tf_op jit(solution)/shard_map/galore_step/pallas_call | solution.py:517
  95.3 0.8 copy.12
  96.0 0.6 copy.13
  96.7 0.6 copy.14
